TPU v7x, 32 devices: a whole 2x2x4 slice. The times are simulated.
32 devices in a mesh: groups: 2 (over y), slab: 16 (over z, x, core).
Axes of the slice: x: 2, y: 2, z: 4, core: 2. Of those that a mesh axis runs over, the one named last changes fastest.
Arguments:
- rhs: float32 [2, 64, 128, 128], P('groups', 'slab'), parts along dimension 0, may hold values from -6 to 6
- labels: int32 [64, 256, 128], P('slab', 'groups'), parts along dimension 1, may hold values from 0 to 4, as said below
- sigma_table: float32 [5, 3], replicated, may hold values from 0.05 to 2
Outputs:
- correction: float32 [2, 64, 128, 128], P('groups', 'slab'), parts along dimension 0
There are 2 independent parts, one for each index of `groups`. A program takes and returns all parts, laid end to end along the dimension named above; an argument that names none is the same for every part. Nothing has to cross between parts.
Inputs may be any that keep to these rules, and one draw needn't show every extreme that they name: Label 0 marks exactly the voxels outside an ellipsoid centred on the grid with semi-axes 0.45 * 128, 0.45 * 128 and 0.55 * 64 cells; inside, labels 1 to 4 are drawn independently for each voxel.
All inputs are finite; a program needn't handle non-finite values.
Results may differ from a plain program's by a relative error of at most 0.0002.
Values sent between devices are 32-bit elements; how exact they have to be, the bound alone decides.
A program may use at most 64 MiB of HBM per device.

v0:
```python
import jax
import jax.numpy as jnp
from jax import lax
from jax.sharding import PartitionSpec as P

LABELS = 5
OMEGA = 0.8


def extended_2(shard, sides, width):
    for axis, dim in sides:
        size, length = (lax.axis_size(axis), shard.shape[dim])
        up = [(i, (i + 1) % size) for i in range(size - 1)]
        down = [(j, i) for i, j in up]
        last = lax.slice_in_dim(shard, length - width, length, axis=dim)
        first = lax.slice_in_dim(shard, 0, width, axis=dim)
        before = lax.ppermute(last, axis, up)
        after = lax.ppermute(first, axis, down)
        shard = jnp.concatenate([before, shard, after], axis=dim)
    return shard


def harmonic(lower_side, upper_side):
    return 2.0 * lower_side * upper_side / (lower_side + upper_side)


def conductivity(padded, sigma_table, column):
    running = jnp.zeros(padded.shape, jnp.float32)
    for tissue in range(LABELS):
        running = running + jnp.where(padded == tissue, sigma_table[tissue, column], 0.0)
    return running


def coefficients(labels_ext, sigma_table):
    padded = jnp.pad(labels_ext, ((0, 0), (1, 1), (1, 1)))
    active = (padded > 0).astype(jnp.float32)
    sigma_x = conductivity(padded, sigma_table, 0)
    sigma_y = conductivity(padded, sigma_table, 1)
    sigma_z = conductivity(padded, sigma_table, 2)
    inner_x = harmonic(sigma_x[1:-1, :-1, 1:-1], sigma_x[1:-1, 1:, 1:-1])
    couple_x = inner_x * active[1:-1, :-1, 1:-1] * active[1:-1, 1:, 1:-1]
    inner_y = harmonic(sigma_y[1:-1, 1:-1, :-1], sigma_y[1:-1, 1:-1, 1:])
    couple_y = inner_y * active[1:-1, 1:-1, :-1] * active[1:-1, 1:-1, 1:]
    inner_z = harmonic(sigma_z[:-1, 1:-1, 1:-1], sigma_z[1:, 1:-1, 1:-1])
    couple_z = inner_z * active[:-1, 1:-1, 1:-1] * active[1:, 1:-1, 1:-1]
    centre_mask = active[1:-1, 1:-1, 1:-1]
    faces = (
        inner_x[:, :-1]
        + inner_x[:, 1:]
        + inner_y[:, :, :-1]
        + inner_y[:, :, 1:]
        + inner_z[:-1]
        + inner_z[1:]
    )
    diagonal = centre_mask * faces + (1.0 - centre_mask)
    return (centre_mask, diagonal, couple_x, couple_y, couple_z)


def operate(extended, terms):
    couple_x, couple_y, couple_z = (terms[2], terms[3], terms[4])
    centre = extended[:, 1:-1]
    widened = jnp.pad(centre, ((0, 0), (0, 0), (1, 1), (1, 1)))
    neighbours = (
        couple_x[:, :-1] * widened[:, :, :-2, 1:-1] + couple_x[:, 1:] * widened[:, :, 2:, 1:-1]
    )
    neighbours = (
        neighbours
        + couple_y[:, :, :-1] * widened[:, :, 1:-1, :-2]
        + couple_y[:, :, 1:] * widened[:, :, 1:-1, 2:]
    )
    neighbours = neighbours + couple_z[:-1] * extended[:, :-2] + couple_z[1:] * extended[:, 2:]
    return terms[1] * centre - neighbours


def smooth(extended, source, terms):
    image = operate(extended, terms)
    return extended[:, 1:-1] + OMEGA * terms[0] * (source - image) / terms[1]


def start(source, terms):
    return OMEGA * terms[0] * source / terms[1]


def leftover(extended, source, terms):
    return terms[0] * (source - operate(extended, terms))


def pair_matrix(length):
    rows_index = lax.broadcasted_iota(jnp.int32, (length, length // 2), 0)
    cols_index = lax.broadcasted_iota(jnp.int32, (length, length // 2), 1)
    return (rows_index // 2 == cols_index).astype(jnp.float32)


def pair_sum(values, along):
    if along == values.ndim - 1:
        return jnp.matmul(values, pair_matrix(values.shape[-1]), precision=lax.Precision.HIGHEST)
    folded = values.shape[:along] + (values.shape[along] // 2, 2) + values.shape[along + 1 :]
    return jnp.sum(values.reshape(folded), axis=along + 1)


def coarsen(terms):
    centre_mask, diagonal, couple_x, couple_y, couple_z = terms
    coarse_x = pair_sum(pair_sum(couple_x[:, 0::2], 0), 2)
    coarse_y = pair_sum(pair_sum(couple_y[:, :, 0::2], 0), 1)
    coarse_z = pair_sum(pair_sum(couple_z[0::2], 1), 2)
    internal = (
        pair_sum(pair_sum(couple_x[:, 1::2], 0), 2)
        + pair_sum(pair_sum(couple_y[:, :, 1::2], 0), 1)
        + pair_sum(pair_sum(couple_z[1::2], 1), 2)
    )
    counted = pair_sum(pair_sum(pair_sum(centre_mask, 0), 1), 2)
    raw_diag = pair_sum(pair_sum(pair_sum(centre_mask * diagonal, 0), 1), 2) - 2.0 * internal
    coarse_mask = jnp.minimum(counted, 1.0)
    coarse_diag = raw_diag + (1.0 - coarse_mask)
    return ((coarse_mask, coarse_diag, coarse_x, coarse_y, coarse_z), raw_diag)


def restrict(field):
    return pair_sum(pair_sum(pair_sum(field, 1), 2), 3)


def widen(field):
    sides, planes, rows_count, cols_count = field.shape
    spread = pair_matrix(2 * cols_count).T
    along_y = jnp.matmul(field, spread, precision=lax.Precision.HIGHEST)
    grown = jnp.broadcast_to(
        along_y[:, :, None, :, None, :], (sides, planes, 2, rows_count, 2, 2 * cols_count)
    )
    return grown.reshape(sides, 2 * planes, 2 * rows_count, 2 * cols_count)


def plane_total(values):
    return jnp.sum(values, axis=(-2, -1))


def line_terms(coarse_terms, raw_diag):
    line_diag = plane_total(raw_diag) - 2.0 * (
        plane_total(coarse_terms[2]) + plane_total(coarse_terms[3])
    )
    return (line_diag, plane_total(coarse_terms[4]))


def fine_rim(field):
    return extended_2(field, (("slab", 1),), 1)


def coarse_rim(field):
    return extended_2(field, (("slab", 1),), 1)


def on_device(rhs, labels, sigma_table):
    labels_near = extended_2(labels, (("slab", 0),), 1)
    own_terms = coefficients(labels_near, sigma_table)
    source = own_terms[0] * rhs
    fine_first = start(source, own_terms)
    fine_second = smooth(fine_rim(fine_first), source, own_terms)
    fine_left = leftover(fine_rim(fine_second), source, own_terms)
    coarse_terms, raw_diag = coarsen(own_terms)
    coarse_source = restrict(fine_left)
    coarse_first = start(coarse_source, coarse_terms)
    coarse_second = smooth(coarse_rim(coarse_first), coarse_source, coarse_terms)
    coarse_left = leftover(coarse_rim(coarse_second), coarse_source, coarse_terms)
    line_diag, line_faces = line_terms(coarse_terms, raw_diag)
    planes = line_diag.shape[0]
    local_rows = plane_total(coarse_left).T
    band = jnp.stack([line_diag, line_faces[:-1]], axis=1)
    all_rows, all_band = (
        lax.all_gather(local_rows, "slab", axis=0, tiled=True),
        lax.all_gather(band, "slab", axis=0, tiled=True),
    )
    lower_band = -all_band[:, 1]
    upper_band = -jnp.concatenate([all_band[1:, 1], jnp.zeros((1,), jnp.float32)])
    line_solution = lax.linalg.tridiagonal_solve(lower_band, all_band[:, 0], upper_band, all_rows)
    own_line = lax.dynamic_slice_in_dim(line_solution, lax.axis_index("slab") * planes, planes, 0)
    coarse_fix = coarse_second + coarse_terms[0] * own_line.T[:, :, None, None]
    coarse_post = smooth(coarse_rim(coarse_fix), coarse_source, coarse_terms)
    coarse_final = smooth(coarse_rim(coarse_post), coarse_source, coarse_terms)
    fine_third = fine_second + own_terms[0] * widen(coarse_final)
    fine_fourth = smooth(fine_rim(fine_third), source, own_terms)
    return smooth(fine_rim(fine_fourth), source, own_terms)


def solution(mesh):
    placed = (P("groups", "slab", None, None), P("slab", "groups", None), P())
    return jax.shard_map(
        on_device,
        mesh=mesh,
        in_specs=placed,
        out_specs=P("groups", "slab", None, None),
        check_vma=False,
    )
```

profile of v0, /device:TPU:8, one launch (start us, length us, event | category | flops | bytes accessed | tf_op | source)
XLA Modules:
  0.0 265.4 jit_solution(3007158552615316442)
XLA Ops:
  0.9 2.7 %collective-permute-start.1 = (s32[1,128,128]{2,1,0:T(8,128)S(1)}, s32[1,128,128]{2,1,0:T(8,128)S(1)}, u32[]{:S(2)}, u32[]{:S(2)}) collective-permute-start(s32[1,128,128]{2,1,0:T(8,128)S(1)} %get-tuple-element.28), channel_id=1, source_target_pairs={{1,0},{2,1},{3,2},{4,3},{5,4},{6,5},{7,6},{8,7},{9,8},{10,9},{11,1... | collective-permute-start | bytes 196616 | tf_op jit(solution)/shard_map/ppermute | solution.py:18
  3.7 1.9 collective-permute-start
  10.5 11.2 %select_add_fusion.2 = (f32[6,130,130]{2,1,0:T(8,128)S(1)}, f32[6,130,130]{2,1,0:T(8,128)}, f32[6,130,130]{2,1,0:T(8,128)S(1)}) fusion(f32[]{:T(128)} %bitcast.6, f32[]{:T(128)} %bitcast.5, f32[]{:T(128)} %bitcast.4, f32[]{:T(128)} %bitcast.3, f32[]{:T(128)} %bitcast.2, s32[6,128,128]{2,1,0:T(8,128)S(1)} %pad_add_fusion, f32[]{:T(128)} %bitcast.16, ...), kind=kLoop, calls=%fused_computation.29 | loop fusion | flops 3244800 | bytes 1610076 | tf_op jit(solution)/shard_map/add | solution.py:30
  28.0 3.3 %collective-permute-start.3 = (f32[1,1,128,128]{3,2,1,0:T(8,128)}, f32[1,1,128,128]{3,2,1,0:T(8,128)}, u32[]{:S(2)}, u32[]{:S(2)}) collective-permute-start(f32[1,1,128,128]{3,2,1,0:T(8,128)} %get-tuple-element.26), channel_id=1, source_target_pairs={{1,0},{2,1},{3,2},{4,3},{5,4},{6,5},{7,6},{8,7},{9,8},{10,9},{11,1... | collective-permute-start | bytes 196616 | tf_op jit(solution)/shard_map/ppermute | solution.py:18
  31.3 1.9 collective-permute-start.2
  33.2 4.6 %slice.1109 = f32[4,128,64]{2,1,0:T(8,128)S(1)} slice(f32[4,128,129]{2,1,0:T(8,128)S(1)} %get-tuple-element.10), slice={[0:4:1], [0:128:1], [1:129:2]} | slice | bytes 262144 | tf_op jit(solution)/shard_map/slice | solution.py:108
  45.9 4.5 %slice.1116 = f32[4,128,65]{2,1,0:T(8,128)S(1)} slice(f32[4,128,129]{2,1,0:T(8,128)S(1)} %get-tuple-element.10), slice={[0:4:1], [0:128:1], [0:129:2]} | slice | bytes 266240 | tf_op jit(solution)/shard_map/slice | solution.py:104
  54.1 4.5 %collective-permute-start.5 = (f32[1,1,128,128]{3,2,1,0:T(8,128)}, f32[1,1,128,128]{3,2,1,0:T(8,128)S(1)}, u32[]{:S(2)}, u32[]{:S(2)}) collective-permute-start(f32[1,1,128,128]{3,2,1,0:T(8,128)} %get-tuple-element.24), channel_id=1, source_target_pairs={{1,0},{2,1},{3,2},{4,3},{5,4},{6,5},{7,6},{8,7},{9,8},{10,9},{11,1... | collective-permute-start | bytes 196616 | tf_op jit(solution)/shard_map/ppermute | solution.py:18
  60.9 4.4 %collective-permute-done.4 = f32[1,1,128,128]{3,2,1,0:T(8,128)S(1)} collective-permute-done((f32[1,1,128,128]{3,2,1,0:T(8,128)}, f32[1,1,128,128]{3,2,1,0:T(8,128)S(1)}, u32[]{:S(2)}, u32[]{:S(2)}) %collective-permute-start.4) | collective-permute-done | bytes 65568 | tf_op jit(solution)/shard_map/ppermute | solution.py:17
  66.9 15.3 %all-gather.1 = f32[16,2,2]{2,1,0:T(2,128)S(1)} all-gather(f32[1,2,2]{2,1,0:T(2,128)S(1)} %bitcast.570), channel_id=1, replica_groups=mesh['groups'=2,'slab'=16] {'slab'}, dimensions={0}, use_global_device_ids=true | all-gather | bytes 272 | tf_op jit(solution)/shard_map/all_gather | solution.py:169
  83.7 6.0 %collective-permute-start.7 = (f32[1,1,64,64]{3,2,1,0:T(8,128)S(1)}, f32[1,1,64,64]{3,2,1,0:T(8,128)S(1)}, u32[]{:S(2)}, u32[]{:S(2)}) collective-permute-start(f32[1,1,64,64]{3,2,1,0:T(8,128)S(1)} %get-tuple-element.40), channel_id=1, source_target_pairs={{1,0},{2,1},{3,2},{4,3},{5,4},{6,5},{7,6},{8,7},{9,8},{10,9},{11,1... | collective-permute-start | bytes 49160 | tf_op jit(solution)/shard_map/ppermute | solution.py:18
  89.7 1.9 collective-permute-start.6
  96.0 2.8 %collective-permute-start.9 = (f32[1,1,64,64]{3,2,1,0:T(8,128)S(1)}, f32[1,1,64,64]{3,2,1,0:T(8,128)S(1)}, u32[]{:S(2)}, u32[]{:S(2)}) collective-permute-start(f32[1,1,64,64]{3,2,1,0:T(8,128)S(1)} %get-tuple-element.36), channel_id=1, source_target_pairs={{1,0},{2,1},{3,2},{4,3},{5,4},{6,5},{7,6},{8,7},{9,8},{10,9},{11,1... | collective-permute-start | bytes 49160 | tf_op jit(solution)/shard_map/ppermute | solution.py:18
  98.7 2.1 collective-permute-start.8
  160.8 24.9 %all-reduce.9 = f32[32]{0:T(128)S(1)} all-reduce(f32[32]{0:T(128)S(1)} %dynamic-update-slice), channel_id=2, replica_groups=mesh['groups'=2,'slab'=16] {'slab'}, use_global_device_ids=true, to_apply=%add.9 | all-reduce | flops 32 | bytes 256
  228.9 1.9 collective-permute-start.11
  230.8 2.4 collective-permute-start.10
  233.2 3.7 %collective-permute-done.10 = f32[1,1,64,64]{3,2,1,0:T(8,128)S(1)} collective-permute-done((f32[1,1,64,64]{3,2,1,0:T(8,128)S(1)}, f32[1,1,64,64]{3,2,1,0:T(8,128)S(1)}, u32[]{:S(2)}, u32[]{:S(2)}) %collective-permute-start.10) | collective-permute-done | bytes 16416 | tf_op jit(solution)/shard_map/ppermute | solution.py:17
  237.1 2.7 %collective-permute-start.13 = (f32[1,1,64,64]{3,2,1,0:T(8,128)S(1)}, f32[1,1,64,64]{3,2,1,0:T(8,128)S(1)}, u32[]{:S(2)}, u32[]{:S(2)}) collective-permute-start(f32[1,1,64,64]{3,2,1,0:T(8,128)S(1)} %get-tuple-element.30), channel_id=1, source_target_pairs={{1,0},{2,1},{3,2},{4,3},{5,4},{6,5},{7,6},{8,7},{9,8},{10,9},{11,1... | collective-permute-start | bytes 49160 | tf_op jit(solution)/shard_map/ppermute | solution.py:18
  241.7 4.8 %collective-permute-done.12 = f32[1,1,64,64]{3,2,1,0:T(8,128)S(1)} collective-permute-done((f32[1,1,64,64]{3,2,1,0:T(8,128)S(1)}, f32[1,1,64,64]{3,2,1,0:T(8,128)S(1)}, u32[]{:S(2)}, u32[]{:S(2)}) %collective-permute-start.12) | collective-permute-done | bytes 16416 | tf_op jit(solution)/shard_map/ppermute | solution.py:17
  249.0 2.4 collective-permute-start.14
  251.4 4.1 %collective-permute-done.14 = f32[1,1,128,128]{3,2,1,0:T(8,128)S(1)} collective-permute-done((f32[1,1,128,128]{3,2,1,0:T(8,128)S(1)}, f32[1,1,128,128]{3,2,1,0:T(8,128)S(1)}, u32[]{:S(2)}, u32[]{:S(2)}) %collective-permute-start.14) | collective-permute-done | bytes 65568 | tf_op jit(solution)/shard_map/ppermute | solution.py:17
  257.9 2.4 collective-permute-start.16
  260.3 4.1 %collective-permute-done.16 = f32[1,1,128,128]{3,2,1,0:T(8,128)S(1)} collective-permute-done((f32[1,1,128,128]{3,2,1,0:T(8,128)S(1)}, f32[1,1,128,128]{3,2,1,0:T(8,128)S(1)}, u32[]{:S(2)}, u32[]{:S(2)}) %collective-permute-start.16) | collective-permute-done | bytes 65568 | tf_op jit(solution)/shard_map/ppermute | solution.py:17
  (132 shorter events, 43.4 us)
Async XLA Ops:
  0.0 10.1 %copy-start.4 = (s32[4,128,128]{2,1,0:T(8,128)S(1)}, s32[4,128,128]{2,1,0:T(8,128)}, u32[]{:S(2)}) copy-start(s32[4,128,128]{2,1,0:T(8,128)} %param.4) | copy-start | bytes 786436
  0.9 8.0 %collective-permute-start.1 = (s32[1,128,128]{2,1,0:T(8,128)S(1)}, s32[1,128,128]{2,1,0:T(8,128)S(1)}, u32[]{:S(2)}, u32[]{:S(2)}) collective-permute-start(s32[1,128,128]{2,1,0:T(8,128)S(1)} %get-tuple-element.28), channel_id=1, source_target_pairs={{1,0},{2,1},{3,2},{4,3},{5,4},{6,5},{7,6},{8,7},{9,8},{10,9},{11,1... | collective-permute-start | bytes 196616 | tf_op jit(solution)/shard_map/ppermute | solution.py:18
  3.7 6.5 %collective-permute-start = (s32[1,128,128]{2,1,0:T(8,128)S(1)}, s32[1,128,128]{2,1,0:T(8,128)S(1)}, u32[]{:S(2)}, u32[]{:S(2)}) collective-permute-start(s32[1,128,128]{2,1,0:T(8,128)S(1)} %get-tuple-element.27), channel_id=1, source_target_pairs={{0,1},{1,2},{2,3},{3,4},{4,5},{5,6},{6,7},{7,8},{8,9},{9,10},{10,1... | collective-permute-start | bytes 196616 | tf_op jit(solution)/shard_map/ppermute | solution.py:17
  28.0 24.2 %collective-permute-start.3 = (f32[1,1,128,128]{3,2,1,0:T(8,128)}, f32[1,1,128,128]{3,2,1,0:T(8,128)}, u32[]{:S(2)}, u32[]{:S(2)}) collective-permute-start(f32[1,1,128,128]{3,2,1,0:T(8,128)} %get-tuple-element.26), channel_id=1, source_target_pairs={{1,0},{2,1},{3,2},{4,3},{5,4},{6,5},{7,6},{8,7},{9,8},{10,9},{11,1... | collective-permute-start | bytes 196616 | tf_op jit(solution)/shard_map/ppermute | solution.py:18
  31.3 20.9 %collective-permute-start.2 = (f32[1,1,128,128]{3,2,1,0:T(8,128)}, f32[1,1,128,128]{3,2,1,0:T(8,128)}, u32[]{:S(2)}, u32[]{:S(2)}) collective-permute-start(f32[1,1,128,128]{3,2,1,0:T(8,128)} %get-tuple-element.25), channel_id=1, source_target_pairs={{0,1},{1,2},{2,3},{3,4},{4,5},{5,6},{6,7},{7,8},{8,9},{9,10},{10,1... | collective-permute-start | bytes 196616 | tf_op jit(solution)/shard_map/ppermute | solution.py:17
  39.8 1.7 copy-start.5
  42.6 1.1 copy-start.3
  45.9 4.6 %copy-start.13 = (f32[2,64,64]{1,2,0:T(8,128)S(1)}, f32[2,64,64]{1,2,0:T(8,128)}, u32[]{:S(2)}) copy-start(f32[2,64,64]{1,2,0:T(8,128)} %get-tuple-element.38) | copy-start | bytes 98308
  54.1 6.9 %collective-permute-start.5 = (f32[1,1,128,128]{3,2,1,0:T(8,128)}, f32[1,1,128,128]{3,2,1,0:T(8,128)S(1)}, u32[]{:S(2)}, u32[]{:S(2)}) collective-permute-start(f32[1,1,128,128]{3,2,1,0:T(8,128)} %get-tuple-element.24), channel_id=1, source_target_pairs={{1,0},{2,1},{3,2},{4,3},{5,4},{6,5},{7,6},{8,7},{9,8},{10,9},{11,1... | collective-permute-start | bytes 196616 | tf_op jit(solution)/shard_map/ppermute | solution.py:18
  58.6 6.7 %collective-permute-start.4 = (f32[1,1,128,128]{3,2,1,0:T(8,128)}, f32[1,1,128,128]{3,2,1,0:T(8,128)S(1)}, u32[]{:S(2)}, u32[]{:S(2)}) collective-permute-start(f32[1,1,128,128]{3,2,1,0:T(8,128)} %get-tuple-element.23), channel_id=1, source_target_pairs={{0,1},{1,2},{2,3},{3,4},{4,5},{5,6},{6,7},{7,8},{8,9},{9,10},{10,1... | collective-permute-start | bytes 196616 | tf_op jit(solution)/shard_map/ppermute | solution.py:17
  83.6 12.2 %copy-start.2 = (f32[2,64,64]{2,1,0:T(8,128)S(1)}, f32[2,64,64]{2,1,0:T(8,128)}, u32[]{:S(2)}) copy-start(f32[2,64,64]{2,1,0:T(8,128)} %copy.35) | copy-start | bytes 98308
  83.7 12.2 %copy-start.1 = (f32[2,64,64]{2,1,0:T(8,128)S(1)}, f32[2,64,64]{2,1,0:T(8,128)}, u32[]{:S(2)}) copy-start(f32[2,64,64]{2,1,0:T(8,128)} %copy.36) | copy-start | bytes 98308
  83.7 10.4 %collective-permute-start.7 = (f32[1,1,64,64]{3,2,1,0:T(8,128)S(1)}, f32[1,1,64,64]{3,2,1,0:T(8,128)S(1)}, u32[]{:S(2)}, u32[]{:S(2)}) collective-permute-start(f32[1,1,64,64]{3,2,1,0:T(8,128)S(1)} %get-tuple-element.40), channel_id=1, source_target_pairs={{1,0},{2,1},{3,2},{4,3},{5,4},{6,5},{7,6},{8,7},{9,8},{10,9},{11,1... | collective-permute-start | bytes 49160 | tf_op jit(solution)/shard_map/ppermute | solution.py:18
  89.7 6.1 %collective-permute-start.6 = (f32[1,1,64,64]{3,2,1,0:T(8,128)S(1)}, f32[1,1,64,64]{3,2,1,0:T(8,128)S(1)}, u32[]{:S(2)}, u32[]{:S(2)}) collective-permute-start(f32[1,1,64,64]{3,2,1,0:T(8,128)S(1)} %get-tuple-element.39), channel_id=1, source_target_pairs={{0,1},{1,2},{2,3},{3,4},{4,5},{5,6},{6,7},{7,8},{8,9},{9,10},{10,1... | collective-permute-start | bytes 49160 | tf_op jit(solution)/shard_map/ppermute | solution.py:17
  96.0 64.4 %collective-permute-start.9 = (f32[1,1,64,64]{3,2,1,0:T(8,128)S(1)}, f32[1,1,64,64]{3,2,1,0:T(8,128)S(1)}, u32[]{:S(2)}, u32[]{:S(2)}) collective-permute-start(f32[1,1,64,64]{3,2,1,0:T(8,128)S(1)} %get-tuple-element.36), channel_id=1, source_target_pairs={{1,0},{2,1},{3,2},{4,3},{5,4},{6,5},{7,6},{8,7},{9,8},{10,9},{11,1... | collective-permute-start | bytes 49160 | tf_op jit(solution)/shard_map/ppermute | solution.py:18
  98.7 61.6 %collective-permute-start.8 = (f32[1,1,64,64]{3,2,1,0:T(8,128)S(1)}, f32[1,1,64,64]{3,2,1,0:T(8,128)S(1)}, u32[]{:S(2)}, u32[]{:S(2)}) collective-permute-start(f32[1,1,64,64]{3,2,1,0:T(8,128)S(1)} %get-tuple-element.35), channel_id=1, source_target_pairs={{0,1},{1,2},{2,3},{3,4},{4,5},{5,6},{6,7},{7,8},{8,9},{9,10},{10,1... | collective-permute-start | bytes 49160 | tf_op jit(solution)/shard_map/ppermute | solution.py:17
  228.9 4.3 %collective-permute-start.11 = (f32[1,1,64,64]{3,2,1,0:T(8,128)S(1)}, f32[1,1,64,64]{3,2,1,0:T(8,128)S(1)}, u32[]{:S(2)}, u32[]{:S(2)}) collective-permute-start(f32[1,1,64,64]{3,2,1,0:T(8,128)S(1)} %get-tuple-element.32), channel_id=1, source_target_pairs={{1,0},{2,1},{3,2},{4,3},{5,4},{6,5},{7,6},{8,7},{9,8},{10,9},{11,1... | collective-permute-start | bytes 49160 | tf_op jit(solution)/shard_map/ppermute | solution.py:18
  230.8 6.1 %collective-permute-start.10 = (f32[1,1,64,64]{3,2,1,0:T(8,128)S(1)}, f32[1,1,64,64]{3,2,1,0:T(8,128)S(1)}, u32[]{:S(2)}, u32[]{:S(2)}) collective-permute-start(f32[1,1,64,64]{3,2,1,0:T(8,128)S(1)} %get-tuple-element.31), channel_id=1, source_target_pairs={{0,1},{1,2},{2,3},{3,4},{4,5},{5,6},{6,7},{7,8},{8,9},{9,10},{10,1... | collective-permute-start | bytes 49160 | tf_op jit(solution)/shard_map/ppermute | solution.py:17
  237.1 4.6 %collective-permute-start.13 = (f32[1,1,64,64]{3,2,1,0:T(8,128)S(1)}, f32[1,1,64,64]{3,2,1,0:T(8,128)S(1)}, u32[]{:S(2)}, u32[]{:S(2)}) collective-permute-start(f32[1,1,64,64]{3,2,1,0:T(8,128)S(1)} %get-tuple-element.30), channel_id=1, source_target_pairs={{1,0},{2,1},{3,2},{4,3},{5,4},{6,5},{7,6},{8,7},{9,8},{10,9},{11,1... | collective-permute-start | bytes 49160 | tf_op jit(solution)/shard_map/ppermute | solution.py:18
  239.8 6.8 %collective-permute-start.12 = (f32[1,1,64,64]{3,2,1,0:T(8,128)S(1)}, f32[1,1,64,64]{3,2,1,0:T(8,128)S(1)}, u32[]{:S(2)}, u32[]{:S(2)}) collective-permute-start(f32[1,1,64,64]{3,2,1,0:T(8,128)S(1)} %get-tuple-element.29), channel_id=1, source_target_pairs={{0,1},{1,2},{2,3},{3,4},{4,5},{5,6},{6,7},{7,8},{8,9},{9,10},{10,1... | collective-permute-start | bytes 49160 | tf_op jit(solution)/shard_map/ppermute | solution.py:17
  247.1 4.3 %collective-permute-start.15 = (f32[1,1,128,128]{3,2,1,0:T(8,128)S(1)}, f32[1,1,128,128]{3,2,1,0:T(8,128)S(1)}, u32[]{:S(2)}, u32[]{:S(2)}) collective-permute-start(f32[1,1,128,128]{3,2,1,0:T(8,128)S(1)} %get-tuple-element.22), channel_id=1, source_target_pairs={{1,0},{2,1},{3,2},{4,3},{5,4},{6,5},{7,6},{8,7},{9,8},{10,9},{11,1... | collective-permute-start | bytes 196616 | tf_op jit(solution)/shard_map/ppermute | solution.py:18
  249.0 6.5 %collective-permute-start.14 = (f32[1,1,128,128]{3,2,1,0:T(8,128)S(1)}, f32[1,1,128,128]{3,2,1,0:T(8,128)S(1)}, u32[]{:S(2)}, u32[]{:S(2)}) collective-permute-start(f32[1,1,128,128]{3,2,1,0:T(8,128)S(1)} %get-tuple-element.21), channel_id=1, source_target_pairs={{0,1},{1,2},{2,3},{3,4},{4,5},{5,6},{6,7},{7,8},{8,9},{9,10},{10,1... | collective-permute-start | bytes 196616 | tf_op jit(solution)/shard_map/ppermute | solution.py:17
  255.9 4.3 %collective-permute-start.17 = (f32[1,1,128,128]{3,2,1,0:T(8,128)S(1)}, f32[1,1,128,128]{3,2,1,0:T(8,128)S(1)}, u32[]{:S(2)}, u32[]{:S(2)}) collective-permute-start(f32[1,1,128,128]{3,2,1,0:T(8,128)S(1)} %get-tuple-element.20), channel_id=1, source_target_pairs={{1,0},{2,1},{3,2},{4,3},{5,4},{6,5},{7,6},{8,7},{9,8},{10,9},{11,1... | collective-permute-start | bytes 196616 | tf_op jit(solution)/shard_map/ppermute | solution.py:18
  257.9 6.5 %collective-permute-start.16 = (f32[1,1,128,128]{3,2,1,0:T(8,128)S(1)}, f32[1,1,128,128]{3,2,1,0:T(8,128)S(1)}, u32[]{:S(2)}, u32[]{:S(2)}) collective-permute-start(f32[1,1,128,128]{3,2,1,0:T(8,128)S(1)} %get-tuple-element.19), channel_id=1, source_target_pairs={{0,1},{1,2},{2,3},{3,4},{4,5},{5,6},{6,7},{7,8},{8,9},{9,10},{10,1... | collective-permute-start | bytes 196616 | tf_op jit(solution)/shard_map/ppermute | solution.py:17
  (10 other events, 8.4 us)
where the time goes:
time: 268 us; the launch traced here: 265 us
  between operations  101 us (38%)
  starting transfers between devices  46.7 us (17%)
  blocking collectives  40.2 us (15%)
  local copies, waits for them, and re-layouts  28.7 us (11%)
  waiting for transfers between devices  24.1 us (9%)
  other arithmetic  21.2 us (8%)
  matrix products  3.07 us (1%)
    ppermute x9, starting transfers between devices, extended_2(): after = lax.ppermute(first, axis, down)  27.8 us
    unnamed x1, blocking collectives  24.9 us
    ppermute x9, waiting for transfers between devices, extended_2(): before = lax.ppermute(last, axis, up)  24.1 us
    ppermute x9, starting transfers between devices, extended_2(): before = lax.ppermute(last, axis, up)  18.9 us
    all_gather x1, blocking collectives, on_device(): lax.all_gather(band, 'slab', axis=0, tiled=True)  15.3 us
    add x1, other arithmetic, conductivity(): running + jnp.where(padded == tissue, sigma_table[tissue, column], 0.0)  11.2 us
    unnamed x39, local copies, waits for them, and re-layouts  7.66 us
    slice x8, local copies, waits for them, and re-layouts, on_device(): lax.linalg.tridiagonal_solve(lower_band, all_band[:, 0], upper_band, all_...  5.56 us
  transfers between devices with their start and end apart: 18, of which 7 were waited for; matrix products, arithmetic and copies ran while one was open for 8% of the time, Pallas kernels for 0%

commit v1 on v0

--- a/solution.py
+++ b/solution.py
@@ -5,6 +5,27 @@
 
 LABELS = 5
 OMEGA = 0.8
+
+
+def gather_around(value, axis, dim):
+    size, mine, extent = (lax.axis_size(axis), lax.axis_index(axis), value.shape[dim])
+    right = [(i, (i + 1) % size) for i in range(size)]
+    left = [(i, (i - 1) % size) for i in range(size)]
+    out = jnp.zeros((*value.shape[:dim], size * extent, *value.shape[dim + 1 :]), value.dtype)
+    out = lax.dynamic_update_slice_in_dim(out, value, mine * extent, axis=dim)
+    from_left = from_right = value
+    half = size // 2
+    for step in range(1, half + 1):
+        from_left = lax.ppermute(from_left, axis, right)
+        out = lax.dynamic_update_slice_in_dim(
+            out, from_left, (mine - step) % size * extent, axis=dim
+        )
+        if step < size - half:
+            from_right = lax.ppermute(from_right, axis, left)
+            out = lax.dynamic_update_slice_in_dim(
+                out, from_right, (mine + step) % size * extent, axis=dim
+            )
+    return out
 
 
 def extended_2(shard, sides, width):
@@ -166,7 +187,7 @@
     band = jnp.stack([line_diag, line_faces[:-1]], axis=1)
     all_rows, all_band = (
         lax.all_gather(local_rows, "slab", axis=0, tiled=True),
-        lax.all_gather(band, "slab", axis=0, tiled=True),
+        gather_around(band, "slab", 0),
     )
     lower_band = -all_band[:, 1]
     upper_band = -jnp.concatenate([all_band[1:, 1], jnp.zeros((1,), jnp.float32)])

time: 268 us -> 287 us (1.071)
  starting transfers between devices: 46.7 us -> 66 us
  blocking collectives: 40.2 us -> 29.6 us
  waiting for transfers between devices: 24.1 us -> 30.6 us
  local copies, waits for them, and re-layouts: 28.7 us -> 31.6 us
    ppermute x0 -> x15, starting transfers between devices: none -> 18.4 us  [the longest x7 18.2 us: gather_around(): from_right = lax.ppermute(from_right, axis, left)]
    all_gather x1 -> x0, blocking collectives: 15.3 us -> none  [on_device(): lax.all_gather(band, 'slab', axis=0, tiled=True)]
    ppermute x0 -> x15, waiting for transfers between devices: none -> 8.79 us  [the longest x8 8.52 us: gather_around(): from_left = lax.ppermute(from_left, axis, right)]
    unnamed x1, blocking collectives: 24.9 us -> 29.6 us
    dynamic_update_slice x0 -> x16, local copies, waits for them, and re-layouts: none -> 3.24 us  [the longest x7 1.61 us: gather_around(): lax.dynamic_update_slice_in_dim(out, from_right, (mine + step) % size * e...]
  transfers between devices with their start and end apart: 18 -> 33, of which waited for: 7 -> 18; matrix products, arithmetic and copies ran while one was open for 8% -> 9% of each run, Pallas kernels for 0% -> 0%
where the time goes in v1:
time: 287 us; the launch traced here: 285 us
  between operations  102 us (36%)
  starting transfers between devices  66 us (23%)
  local copies, waits for them, and re-layouts  31.6 us (11%)
  waiting for transfers between devices  30.6 us (11%)
  blocking collectives  29.6 us (10%)
  other arithmetic  21.9 us (8%)
  matrix products  3.07 us (1%)
    unnamed x1, blocking collectives  29.6 us
    ppermute x9, starting transfers between devices, extended_2(): after = lax.ppermute(first, axis, down)  28.5 us
    ppermute x9, waiting for transfers between devices, extended_2(): before = lax.ppermute(last, axis, up)  21.8 us
    ppermute x9, starting transfers between devices, extended_2(): before = lax.ppermute(last, axis, up)  19.2 us
    ppermute x7, starting transfers between devices, gather_around(): from_right = lax.ppermute(from_right, axis, left)  18.2 us
    add x1, other arithmetic, conductivity(): running + jnp.where(padded == tissue, sigma_table[tissue, column], 0.0)  11.2 us
    ppermute x8, waiting for transfers between devices, gather_around(): from_left = lax.ppermute(from_left, axis, right)  8.52 us
    unnamed x39, local copies, waits for them, and re-layouts  7.43 us
  transfers between devices with their start and end apart: 33, of which 18 were waited for; matrix products, arithmetic and copies ran while one was open for 9% of the time, Pallas kernels for 0%

profile of v1, /device:TPU:8, one launch (start us, length us, event | category | flops | bytes accessed | tf_op | source)
XLA Modules:
  0.0 284.6 jit_solution(8431064376320469304)
XLA Ops:
  0.9 2.9 %collective-permute-start.1 = (s32[1,128,128]{2,1,0:T(8,128)S(1)}, s32[1,128,128]{2,1,0:T(8,128)S(1)}, u32[]{:S(2)}, u32[]{:S(2)}) collective-permute-start(s32[1,128,128]{2,1,0:T(8,128)S(1)} %get-tuple-element.28), channel_id=1, source_target_pairs={{1,0},{2,1},{3,2},{4,3},{5,4},{6,5},{7,6},{8,7},{9,8},{10,9},{11,1... | collective-permute-start | bytes 196616 | tf_op jit(solution)/shard_map/ppermute | solution.py:39
  10.6 11.2 %select_add_fusion.2 = (f32[6,130,130]{2,1,0:T(8,128)S(1)}, f32[6,130,130]{2,1,0:T(8,128)}, f32[6,130,130]{2,1,0:T(8,128)S(1)}) fusion(f32[]{:T(128)} %bitcast.6, f32[]{:T(128)} %bitcast.5, f32[]{:T(128)} %bitcast.4, f32[]{:T(128)} %bitcast.3, f32[]{:T(128)} %bitcast.2, s32[6,128,128]{2,1,0:T(8,128)S(1)} %pad_add_fusion, f32[]{:T(128)} %bitcast.16, ...), kind=kLoop, calls=%fused_computation.29 | loop fusion | flops 3244800 | bytes 1610076 | tf_op jit(solution)/shard_map/add | solution.py:51
  28.1 3.6 %collective-permute-start.3 = (f32[1,1,128,128]{3,2,1,0:T(8,128)}, f32[1,1,128,128]{3,2,1,0:T(8,128)}, u32[]{:S(2)}, u32[]{:S(2)}) collective-permute-start(f32[1,1,128,128]{3,2,1,0:T(8,128)} %get-tuple-element.26), channel_id=1, source_target_pairs={{1,0},{2,1},{3,2},{4,3},{5,4},{6,5},{7,6},{8,7},{9,8},{10,9},{11,1... | collective-permute-start | bytes 196616 | tf_op jit(solution)/shard_map/ppermute | solution.py:39
  33.7 4.6 %slice.1109 = f32[4,128,64]{2,1,0:T(8,128)S(1)} slice(f32[4,128,129]{2,1,0:T(8,128)S(1)} %get-tuple-element.10), slice={[0:4:1], [0:128:1], [1:129:2]} | slice | bytes 262144 | tf_op jit(solution)/shard_map/slice | solution.py:129
  46.9 4.5 %slice.1116 = f32[4,128,65]{2,1,0:T(8,128)S(1)} slice(f32[4,128,129]{2,1,0:T(8,128)S(1)} %get-tuple-element.10), slice={[0:4:1], [0:128:1], [0:129:2]} | slice | bytes 266240 | tf_op jit(solution)/shard_map/slice | solution.py:125
  55.1 4.5 %collective-permute-start.5 = (f32[1,1,128,128]{3,2,1,0:T(8,128)}, f32[1,1,128,128]{3,2,1,0:T(8,128)S(1)}, u32[]{:S(2)}, u32[]{:S(2)}) collective-permute-start(f32[1,1,128,128]{3,2,1,0:T(8,128)} %get-tuple-element.24), channel_id=1, source_target_pairs={{1,0},{2,1},{3,2},{4,3},{5,4},{6,5},{7,6},{8,7},{9,8},{10,9},{11,1... | collective-permute-start | bytes 196616 | tf_op jit(solution)/shard_map/ppermute | solution.py:39
  61.9 4.4 %collective-permute-done.4 = f32[1,1,128,128]{3,2,1,0:T(8,128)S(1)} collective-permute-done((f32[1,1,128,128]{3,2,1,0:T(8,128)}, f32[1,1,128,128]{3,2,1,0:T(8,128)S(1)}, u32[]{:S(2)}, u32[]{:S(2)}) %collective-permute-start.4) | collective-permute-done | bytes 65568 | tf_op jit(solution)/shard_map/ppermute | solution.py:38
  67.9 2.6 collective-permute-start.11
  75.2 2.6 collective-permute-start.13
  79.1 2.6 collective-permute-start.15
  83.0 2.6 collective-permute-start.17
  86.9 2.6 collective-permute-start.19
  90.8 2.6 collective-permute-start.21
  94.7 2.6 collective-permute-start.23
  99.0 3.4 %collective-permute-done.24 = f32[2,2]{0,1:T(2,128)S(1)} collective-permute-done((f32[2,2]{0,1:T(2,128)S(1)}, f32[2,2]{0,1:T(2,128)S(1)}, u32[]{:S(2)}, u32[]{:S(2)}) %collective-permute-start.24) | collective-permute-done | bytes 48 | tf_op jit(solution)/shard_map/ppermute | solution.py:19
  108.5 2.4 collective-permute-start.8
  170.9 29.6 %all-reduce.9 = f32[32]{0:T(128)S(1)} all-reduce(f32[32]{0:T(128)S(1)} %dynamic-update-slice), channel_id=2, replica_groups=mesh['groups'=2,'slab'=16] {'slab'}, use_global_device_ids=true, to_apply=%add.9 | all-reduce | flops 32 | bytes 256
  243.5 6.3 %collective-permute-start.26 = (f32[1,1,64,64]{3,2,1,0:T(8,128)S(1)}, f32[1,1,64,64]{3,2,1,0:T(8,128)S(1)}, u32[]{:S(2)}, u32[]{:S(2)}) collective-permute-start(f32[1,1,64,64]{3,2,1,0:T(8,128)S(1)} %get-tuple-element.32), channel_id=1, source_target_pairs={{1,0},{2,1},{3,2},{4,3},{5,4},{6,5},{7,6},{8,7},{9,8},{10,9},{11,1... | collective-permute-start | bytes 49160 | tf_op jit(solution)/shard_map/ppermute | solution.py:39
  251.8 4.2 %collective-permute-done.25 = f32[1,1,64,64]{3,2,1,0:T(8,128)S(1)} collective-permute-done((f32[1,1,64,64]{3,2,1,0:T(8,128)S(1)}, f32[1,1,64,64]{3,2,1,0:T(8,128)S(1)}, u32[]{:S(2)}, u32[]{:S(2)}) %collective-permute-start.25) | collective-permute-done | bytes 16416 | tf_op jit(solution)/shard_map/ppermute | solution.py:38
  256.1 3.5 %collective-permute-start.28 = (f32[1,1,64,64]{3,2,1,0:T(8,128)S(1)}, f32[1,1,64,64]{3,2,1,0:T(8,128)S(1)}, u32[]{:S(2)}, u32[]{:S(2)}) collective-permute-start(f32[1,1,64,64]{3,2,1,0:T(8,128)S(1)} %get-tuple-element.30), channel_id=1, source_target_pairs={{1,0},{2,1},{3,2},{4,3},{5,4},{6,5},{7,6},{8,7},{9,8},{10,9},{11,1... | collective-permute-start | bytes 49160 | tf_op jit(solution)/shard_map/ppermute | solution.py:39
  261.5 4.2 %collective-permute-done.27 = f32[1,1,64,64]{3,2,1,0:T(8,128)S(1)} collective-permute-done((f32[1,1,64,64]{3,2,1,0:T(8,128)S(1)}, f32[1,1,64,64]{3,2,1,0:T(8,128)S(1)}, u32[]{:S(2)}, u32[]{:S(2)}) %collective-permute-start.27) | collective-permute-done | bytes 16416 | tf_op jit(solution)/shard_map/ppermute | solution.py:38
  268.2 2.4 collective-permute-start.29
  270.6 4.1 %collective-permute-done.29 = f32[1,1,128,128]{3,2,1,0:T(8,128)S(1)} collective-permute-done((f32[1,1,128,128]{3,2,1,0:T(8,128)S(1)}, f32[1,1,128,128]{3,2,1,0:T(8,128)S(1)}, u32[]{:S(2)}, u32[]{:S(2)}) %collective-permute-start.29) | collective-permute-done | bytes 65568 | tf_op jit(solution)/shard_map/ppermute | solution.py:38
  279.4 4.1 %collective-permute-done.31 = f32[1,1,128,128]{3,2,1,0:T(8,128)S(1)} collective-permute-done((f32[1,1,128,128]{3,2,1,0:T(8,128)S(1)}, f32[1,1,128,128]{3,2,1,0:T(8,128)S(1)}, u32[]{:S(2)}, u32[]{:S(2)}) %collective-permute-start.31) | collective-permute-done | bytes 65568 | tf_op jit(solution)/shard_map/ppermute | solution.py:38
  (176 shorter events, 64.7 us)
Async XLA Ops:
  0.9 8.4 %collective-permute-start.1 = (s32[1,128,128]{2,1,0:T(8,128)S(1)}, s32[1,128,128]{2,1,0:T(8,128)S(1)}, u32[]{:S(2)}, u32[]{:S(2)}) collective-permute-start(s32[1,128,128]{2,1,0:T(8,128)S(1)} %get-tuple-element.28), channel_id=1, source_target_pairs={{1,0},{2,1},{3,2},{4,3},{5,4},{6,5},{7,6},{8,7},{9,8},{10,9},{11,1... | collective-permute-start | bytes 196616 | tf_op jit(solution)/shard_map/ppermute | solution.py:39
  3.8 6.5 %collective-permute-start = (s32[1,128,128]{2,1,0:T(8,128)S(1)}, s32[1,128,128]{2,1,0:T(8,128)S(1)}, u32[]{:S(2)}, u32[]{:S(2)}) collective-permute-start(s32[1,128,128]{2,1,0:T(8,128)S(1)} %get-tuple-element.27), channel_id=1, source_target_pairs={{0,1},{1,2},{2,3},{3,4},{4,5},{5,6},{6,7},{7,8},{8,9},{9,10},{10,1... | collective-permute-start | bytes 196616 | tf_op jit(solution)/shard_map/ppermute | solution.py:38
  28.1 25.1 %collective-permute-start.3 = (f32[1,1,128,128]{3,2,1,0:T(8,128)}, f32[1,1,128,128]{3,2,1,0:T(8,128)}, u32[]{:S(2)}, u32[]{:S(2)}) collective-permute-start(f32[1,1,128,128]{3,2,1,0:T(8,128)} %get-tuple-element.26), channel_id=1, source_target_pairs={{1,0},{2,1},{3,2},{4,3},{5,4},{6,5},{7,6},{8,7},{9,8},{10,9},{11,1... | collective-permute-start | bytes 196616 | tf_op jit(solution)/shard_map/ppermute | solution.py:39
  31.7 21.5 %collective-permute-start.2 = (f32[1,1,128,128]{3,2,1,0:T(8,128)}, f32[1,1,128,128]{3,2,1,0:T(8,128)}, u32[]{:S(2)}, u32[]{:S(2)}) collective-permute-start(f32[1,1,128,128]{3,2,1,0:T(8,128)} %get-tuple-element.25), channel_id=1, source_target_pairs={{0,1},{1,2},{2,3},{3,4},{4,5},{5,6},{6,7},{7,8},{8,9},{9,10},{10,1... | collective-permute-start | bytes 196616 | tf_op jit(solution)/shard_map/ppermute | solution.py:38
  55.1 6.9 %collective-permute-start.5 = (f32[1,1,128,128]{3,2,1,0:T(8,128)}, f32[1,1,128,128]{3,2,1,0:T(8,128)S(1)}, u32[]{:S(2)}, u32[]{:S(2)}) collective-permute-start(f32[1,1,128,128]{3,2,1,0:T(8,128)} %get-tuple-element.24), channel_id=1, source_target_pairs={{1,0},{2,1},{3,2},{4,3},{5,4},{6,5},{7,6},{8,7},{9,8},{10,9},{11,1... | collective-permute-start | bytes 196616 | tf_op jit(solution)/shard_map/ppermute | solution.py:39
  59.6 6.7 %collective-permute-start.4 = (f32[1,1,128,128]{3,2,1,0:T(8,128)}, f32[1,1,128,128]{3,2,1,0:T(8,128)S(1)}, u32[]{:S(2)}, u32[]{:S(2)}) collective-permute-start(f32[1,1,128,128]{3,2,1,0:T(8,128)} %get-tuple-element.23), channel_id=1, source_target_pairs={{0,1},{1,2},{2,3},{3,4},{4,5},{5,6},{6,7},{7,8},{8,9},{9,10},{10,1... | collective-permute-start | bytes 196616 | tf_op jit(solution)/shard_map/ppermute | solution.py:38
  67.8 7.3 %collective-permute-start.10 = (f32[2,2]{0,1:T(2,128)S(1)}, f32[2,2]{0,1:T(2,128)S(1)}, u32[]{:S(2)}, u32[]{:S(2)}) collective-permute-start(f32[2,2]{0,1:T(2,128)S(1)} %pad_maximum_fusion.16), channel_id=1, source_target_pairs={{0,1},{1,2},{2,3},{3,4},{4,5},{5,6},{6,7},{7,8},{8,9},{9,10},{10,1... | collective-permute-start | bytes 56 | tf_op jit(solution)/shard_map/ppermute | solution.py:19
  67.9 7.3 %collective-permute-start.11 = (f32[2,2]{0,1:T(2,128)S(1)}, f32[2,2]{0,1:T(2,128)S(1)}, u32[]{:S(2)}, u32[]{:S(2)}) collective-permute-start(f32[2,2]{0,1:T(2,128)S(1)} %pad_maximum_fusion.16), channel_id=1, source_target_pairs={{0,15},{1,0},{2,1},{3,2},{4,3},{5,4},{6,5},{7,6},{8,7},{9,8},{10,9... | collective-permute-start | bytes 56 | tf_op jit(solution)/shard_map/ppermute | solution.py:24
  70.5 35.8 %collective-permute-start.7 = (f32[1,1,64,64]{3,2,1,0:T(8,128)S(1)}, f32[1,1,64,64]{3,2,1,0:T(8,128)S(1)}, u32[]{:S(2)}, u32[]{:S(2)}) collective-permute-start(f32[1,1,64,64]{3,2,1,0:T(8,128)S(1)} %get-tuple-element.40), channel_id=1, source_target_pairs={{1,0},{2,1},{3,2},{4,3},{5,4},{6,5},{7,6},{8,7},{9,8},{10,9},{11,1... | collective-permute-start | bytes 49160 | tf_op jit(solution)/shard_map/ppermute | solution.py:39
  72.4 33.9 %collective-permute-start.6 = (f32[1,1,64,64]{3,2,1,0:T(8,128)S(1)}, f32[1,1,64,64]{3,2,1,0:T(8,128)S(1)}, u32[]{:S(2)}, u32[]{:S(2)}) collective-permute-start(f32[1,1,64,64]{3,2,1,0:T(8,128)S(1)} %get-tuple-element.39), channel_id=1, source_target_pairs={{0,1},{1,2},{2,3},{3,4},{4,5},{5,6},{6,7},{7,8},{8,9},{9,10},{10,1... | collective-permute-start | bytes 49160 | tf_op jit(solution)/shard_map/ppermute | solution.py:38
  75.1 3.9 %collective-permute-start.12 = (f32[2,2]{0,1:T(2,128)S(1)}, f32[2,2]{0,1:T(2,128)S(1)}, u32[]{:S(2)}, u32[]{:S(2)}) collective-permute-start(f32[2,2]{0,1:T(2,128)S(1)} %collective-permute-done.10), channel_id=1, source_target_pairs={{0,1},{1,2},{2,3},{3,4},{4,5},{5,6},{6,7},{7,8},{8,9},{9,10},{10,1... | collective-permute-start | bytes 56 | tf_op jit(solution)/shard_map/ppermute | solution.py:19
  75.2 3.9 %collective-permute-start.13 = (f32[2,2]{0,1:T(2,128)S(1)}, f32[2,2]{0,1:T(2,128)S(1)}, u32[]{:S(2)}, u32[]{:S(2)}) collective-permute-start(f32[2,2]{0,1:T(2,128)S(1)} %collective-permute-done.11), channel_id=1, source_target_pairs={{0,15},{1,0},{2,1},{3,2},{4,3},{5,4},{6,5},{7,6},{8,7},{9,8},{10,9... | collective-permute-start | bytes 56 | tf_op jit(solution)/shard_map/ppermute | solution.py:24
  79.1 3.9 %collective-permute-start.14 = (f32[2,2]{0,1:T(2,128)S(1)}, f32[2,2]{0,1:T(2,128)S(1)}, u32[]{:S(2)}, u32[]{:S(2)}) collective-permute-start(f32[2,2]{0,1:T(2,128)S(1)} %collective-permute-done.12), channel_id=1, source_target_pairs={{0,1},{1,2},{2,3},{3,4},{4,5},{5,6},{6,7},{7,8},{8,9},{9,10},{10,1... | collective-permute-start | bytes 56 | tf_op jit(solution)/shard_map/ppermute | solution.py:19
  94.7 4.0 %collective-permute-start.23 = (f32[2,2]{0,1:T(2,128)S(1)}, f32[2,2]{0,1:T(2,128)S(1)}, u32[]{:S(2)}, u32[]{:S(2)}) collective-permute-start(f32[2,2]{0,1:T(2,128)S(1)} %collective-permute-done.21), channel_id=1, source_target_pairs={{0,15},{1,0},{2,1},{3,2},{4,3},{5,4},{6,5},{7,6},{8,7},{9,8},{10,9... | collective-permute-start | bytes 56 | tf_op jit(solution)/shard_map/ppermute | solution.py:24
  106.5 63.9 %collective-permute-start.9 = (f32[1,1,64,64]{3,2,1,0:T(8,128)S(1)}, f32[1,1,64,64]{3,2,1,0:T(8,128)S(1)}, u32[]{:S(2)}, u32[]{:S(2)}) collective-permute-start(f32[1,1,64,64]{3,2,1,0:T(8,128)S(1)} %get-tuple-element.36), channel_id=1, source_target_pairs={{1,0},{2,1},{3,2},{4,3},{5,4},{6,5},{7,6},{8,7},{9,8},{10,9},{11,1... | collective-permute-start | bytes 49160 | tf_op jit(solution)/shard_map/ppermute | solution.py:39
  108.5 62.0 %collective-permute-start.8 = (f32[1,1,64,64]{3,2,1,0:T(8,128)S(1)}, f32[1,1,64,64]{3,2,1,0:T(8,128)S(1)}, u32[]{:S(2)}, u32[]{:S(2)}) collective-permute-start(f32[1,1,64,64]{3,2,1,0:T(8,128)S(1)} %get-tuple-element.35), channel_id=1, source_target_pairs={{0,1},{1,2},{2,3},{3,4},{4,5},{5,6},{6,7},{7,8},{8,9},{9,10},{10,1... | collective-permute-start | bytes 49160 | tf_op jit(solution)/shard_map/ppermute | solution.py:38
  243.5 8.3 %collective-permute-start.26 = (f32[1,1,64,64]{3,2,1,0:T(8,128)S(1)}, f32[1,1,64,64]{3,2,1,0:T(8,128)S(1)}, u32[]{:S(2)}, u32[]{:S(2)}) collective-permute-start(f32[1,1,64,64]{3,2,1,0:T(8,128)S(1)} %get-tuple-element.32), channel_id=1, source_target_pairs={{1,0},{2,1},{3,2},{4,3},{5,4},{6,5},{7,6},{8,7},{9,8},{10,9},{11,1... | collective-permute-start | bytes 49160 | tf_op jit(solution)/shard_map/ppermute | solution.py:39
  249.8 6.1 %collective-permute-start.25 = (f32[1,1,64,64]{3,2,1,0:T(8,128)S(1)}, f32[1,1,64,64]{3,2,1,0:T(8,128)S(1)}, u32[]{:S(2)}, u32[]{:S(2)}) collective-permute-start(f32[1,1,64,64]{3,2,1,0:T(8,128)S(1)} %get-tuple-element.31), channel_id=1, source_target_pairs={{0,1},{1,2},{2,3},{3,4},{4,5},{5,6},{6,7},{7,8},{8,9},{9,10},{10,1... | collective-permute-start | bytes 49160 | tf_op jit(solution)/shard_map/ppermute | solution.py:38
  256.1 5.4 %collective-permute-start.28 = (f32[1,1,64,64]{3,2,1,0:T(8,128)S(1)}, f32[1,1,64,64]{3,2,1,0:T(8,128)S(1)}, u32[]{:S(2)}, u32[]{:S(2)}) collective-permute-start(f32[1,1,64,64]{3,2,1,0:T(8,128)S(1)} %get-tuple-element.30), channel_id=1, source_target_pairs={{1,0},{2,1},{3,2},{4,3},{5,4},{6,5},{7,6},{8,7},{9,8},{10,9},{11,1... | collective-permute-start | bytes 49160 | tf_op jit(solution)/shard_map/ppermute | solution.py:39
  259.6 6.1 %collective-permute-start.27 = (f32[1,1,64,64]{3,2,1,0:T(8,128)S(1)}, f32[1,1,64,64]{3,2,1,0:T(8,128)S(1)}, u32[]{:S(2)}, u32[]{:S(2)}) collective-permute-start(f32[1,1,64,64]{3,2,1,0:T(8,128)S(1)} %get-tuple-element.29), channel_id=1, source_target_pairs={{0,1},{1,2},{2,3},{3,4},{4,5},{5,6},{6,7},{7,8},{8,9},{9,10},{10,1... | collective-permute-start | bytes 49160 | tf_op jit(solution)/shard_map/ppermute | solution.py:38
  266.2 4.3 %collective-permute-start.30 = (f32[1,1,128,128]{3,2,1,0:T(8,128)S(1)}, f32[1,1,128,128]{3,2,1,0:T(8,128)S(1)}, u32[]{:S(2)}, u32[]{:S(2)}) collective-permute-start(f32[1,1,128,128]{3,2,1,0:T(8,128)S(1)} %get-tuple-element.22), channel_id=1, source_target_pairs={{1,0},{2,1},{3,2},{4,3},{5,4},{6,5},{7,6},{8,7},{9,8},{10,9},{11,1... | collective-permute-start | bytes 196616 | tf_op jit(solution)/shard_map/ppermute | solution.py:39
  268.2 6.5 %collective-permute-start.29 = (f32[1,1,128,128]{3,2,1,0:T(8,128)S(1)}, f32[1,1,128,128]{3,2,1,0:T(8,128)S(1)}, u32[]{:S(2)}, u32[]{:S(2)}) collective-permute-start(f32[1,1,128,128]{3,2,1,0:T(8,128)S(1)} %get-tuple-element.21), channel_id=1, source_target_pairs={{0,1},{1,2},{2,3},{3,4},{4,5},{5,6},{6,7},{7,8},{8,9},{9,10},{10,1... | collective-permute-start | bytes 196616 | tf_op jit(solution)/shard_map/ppermute | solution.py:38
  275.1 4.3 %collective-permute-start.32 = (f32[1,1,128,128]{3,2,1,0:T(8,128)S(1)}, f32[1,1,128,128]{3,2,1,0:T(8,128)S(1)}, u32[]{:S(2)}, u32[]{:S(2)}) collective-permute-start(f32[1,1,128,128]{3,2,1,0:T(8,128)S(1)} %get-tuple-element.20), channel_id=1, source_target_pairs={{1,0},{2,1},{3,2},{4,3},{5,4},{6,5},{7,6},{8,7},{9,8},{10,9},{11,1... | collective-permute-start | bytes 196616 | tf_op jit(solution)/shard_map/ppermute | solution.py:39
  277.0 6.5 %collective-permute-start.31 = (f32[1,1,128,128]{3,2,1,0:T(8,128)S(1)}, f32[1,1,128,128]{3,2,1,0:T(8,128)S(1)}, u32[]{:S(2)}, u32[]{:S(2)}) collective-permute-start(f32[1,1,128,128]{3,2,1,0:T(8,128)S(1)} %get-tuple-element.19), channel_id=1, source_target_pairs={{0,1},{1,2},{2,3},{3,4},{4,5},{5,6},{6,7},{7,8},{8,9},{9,10},{10,1... | collective-permute-start | bytes 196616 | tf_op jit(solution)/shard_map/ppermute | solution.py:38
  (26 other events, 116.7 us)
